TPU v7x, 32 devices: a whole 2x2x4 slice. The times are simulated.
32 devices in a mesh: groups: 2 (over x), gx: 4 (over y, core), gy: 4 (over z).
Axes of the slice: x: 2, y: 2, z: 4, core: 2. Of those that a mesh axis runs over, the one named last changes fastest.
Arguments:
- tokens: bfloat16 [64, 2, 16384], P('groups', None, 'gx'), parts along dimension 0
- norm_gain: bfloat16 [16384], P('gx'), may hold values from 0.099609375 to 1.8984375
- qkv_weight: bfloat16 [16384, 8, 18, 128], P('gx', 'gy'), may hold values from -0.046875 to 0.046875
- out_weight: bfloat16 [128, 128, 16384], P('gy', None, 'gx'), may hold values from -0.125 to 0.125
- kv_cache: bfloat16 [64, 384, 2, 8, 128], P(('groups', 'gx', 'gy')), parts along dimension 0
- lengths: int32 [64], P(('groups', 'gx', 'gy')), parts along dimension 0, may hold values from 1 to 384, as said below
- positions: int32 [64], P('groups'), parts along dimension 0, may hold values from 0 to 4095
Outputs:
- layer_out: float32 [64, 2, 16384], P(('groups', 'gy'), None, 'gx'), parts along dimension 0
There are 2 independent parts, one for each index of `groups`. A program takes and returns all parts, laid end to end along the dimension named above; an argument that names none is the same for every part. Nothing has to cross between parts.
Inputs may be any that keep to these rules, and one draw needn't show every extreme that they name: Cache slots 0 to lengths - 1 of a row hold its earlier tokens; some row has exactly 384.
All inputs are finite; a program needn't handle non-finite values.
Results may differ from a plain program's by a relative error of at most 0.025.
Values may be sent and summed in bfloat16 or wider, within the bound.
A program may use at most 192 MiB of HBM per device.

v0:
```python
import functools
import math

import jax
import jax.numpy as jnp
from jax import lax
from jax.experimental import pallas as pl
from jax.experimental.pallas import tpu as pltpu
from jax.sharding import PartitionSpec as P

D = 16384


norm_eps = 1e-05
rope_base = 500000.0


def rotate(values, places):
    half_dim = values.shape[-1] // 2
    index_half = jnp.arange(half_dim, dtype=jnp.float32)
    frequency = rope_base ** (-2.0 * index_half / values.shape[-1])
    angles = places[..., None] * frequency
    cosine = jnp.cos(angles)
    sine_part = jnp.sin(angles)
    front_half = values[..., :half_dim]
    back_half = values[..., half_dim:]
    return jnp.concatenate(
        [front_half * cosine - back_half * sine_part, back_half * cosine + front_half * sine_part],
        axis=-1,
    )


def finish(projected, positions, first_row, row_count):
    group_size = projected.shape[3] - 2
    placed = lax.dynamic_slice_in_dim(positions, first_row, row_count, 0)
    places = (placed[:, None] + jnp.arange(2, dtype=jnp.int32)[None, :]).astype(jnp.float32)
    queries = rotate(projected[:, :, :, :group_size], places[:, :, None, None])
    key_new = rotate(projected[:, :, :, group_size : group_size + 1], places[:, :, None, None])
    value_new = projected[:, :, :, group_size + 1 :]
    return jnp.concatenate([queries, key_new, value_new], axis=3).astype(jnp.bfloat16)


def attend(queries, key_new, value_new, cache_rows, length):
    scale_factor = 1.0 / math.sqrt(queries.shape[-1])
    scores_old = (
        jnp.einsum(
            "rtgid,rsgd->rtgis", queries, cache_rows[:, :, 0], preferred_element_type=jnp.float32
        )
        * scale_factor
    )
    slot_ids = jnp.arange(cache_rows.shape[1], dtype=jnp.int32)
    visible = slot_ids[None, :] < length[:, None]
    scores_old = jnp.where(visible[:, None, None, None, :], scores_old, -1e30)
    scores_new = (
        jnp.einsum("rtgid,rugd->rtgiu", queries, key_new, preferred_element_type=jnp.float32)
        * scale_factor
    )
    token_ids = jnp.arange(queries.shape[1], dtype=jnp.int32)
    causal = token_ids[:, None] >= token_ids[None, :]
    scores_new = jnp.where(causal[None, :, None, None, :], scores_new, -1e30)
    highest = jnp.maximum(jnp.max(scores_old, axis=-1), jnp.max(scores_new, axis=-1))
    expo_old = jnp.exp(scores_old - highest[..., None])
    expo_new = jnp.exp(scores_new - highest[..., None])
    denominator = jnp.sum(expo_old, axis=-1) + jnp.sum(expo_new, axis=-1)
    weight_old = (expo_old / denominator[..., None]).astype(jnp.bfloat16)
    weight_new = (expo_new / denominator[..., None]).astype(jnp.bfloat16)
    attended = jnp.einsum(
        "rtgis,rsgd->rtgid", weight_old, cache_rows[:, :, 1], preferred_element_type=jnp.float32
    )
    attended = attended + jnp.einsum(
        "rtgiu,rugd->rtgid", weight_new, value_new, preferred_element_type=jnp.float32
    )
    return attended.astype(jnp.bfloat16)


def bring(weight_ref, chunk_ref, sems, first):
    copies = [
        pltpu.make_async_copy(weight_ref.at[:, first + at], chunk_ref.at[at], sems.at[at])
        for at in range(chunk_ref.shape[0])
    ]
    for copy in copies:
        copy.start()
    return copies


def open_kernel(block_rows, depth, tokens_ref, gain_ref, weight_ref, left_ref, extra_ref, chunk_ref, sems):
    groups = 2
    total_tokens, local_width = tokens_ref.shape
    copies = bring(weight_ref, chunk_ref, sems, 0)
    feature = lax.broadcasted_iota(jnp.int32, (128, 256), 0)
    target = lax.broadcasted_iota(jnp.int32, (128, 256), 1)
    spreads = [
        jnp.where(target == feature * groups + group, 1.0, 0.0).astype(jnp.bfloat16)
        for group in range(groups)
    ]

    def order(pieces):
        return jnp.concatenate(
            [
                pieces[group][row : row + block_rows]
                for row in range(0, total_tokens, block_rows)
                for group in range(groups)
            ],
            axis=0,
        )

    def step(at, squares):
        start = pl.multiple_of(at * depth, depth)
        wide = tokens_ref[:, pl.ds(start, depth)].astype(jnp.float32)
        hidden = (wide * gain_ref[:, pl.ds(start, depth)].astype(jnp.float32)).astype(jnp.bfloat16)
        for near in range(0, depth, 128):
            squares += wide[:, near : near + 128] * wide[:, near : near + 128]
            spread = [
                jnp.dot(
                    hidden[:, near : near + 128], spreads[group], preferred_element_type=jnp.float32
                ).astype(jnp.bfloat16)
                for group in range(groups)
            ]
            begin = pl.multiple_of((start + near) * groups, 256)
            left_ref[:, pl.ds(begin, 256)] = order(spread)
        return squares

    squares = lax.fori_loop(
        0, local_width // depth, step, jnp.zeros((total_tokens, 128), jnp.float32)
    )
    summed = jnp.sum(squares, axis=1, keepdims=True)
    coarse = summed.astype(jnp.bfloat16).astype(jnp.float32)
    lane = lax.broadcasted_iota(jnp.int32, (total_tokens, 128), 1)
    extra = jnp.where(lane < 64, coarse, summed - coarse)
    extra_ref[...] = order([extra, extra]).astype(jnp.bfloat16)
    for copy in copies:
        copy.wait()


def multiply_kernel(following, left_ref, chunk_ref, weight_ref, out_ref, *rest):
    copies = []
    if following is not None:
        next_ref, total, sems = rest
        copies = bring(weight_ref, next_ref, sems, following)
    else:
        (total,) = rest
    count, contraction, head_dim = chunk_ref.shape
    total[...] = jnp.zeros_like(total)

    @pl.loop(0, contraction // 1024)
    def _(step):
        span = pl.ds(pl.multiple_of(step * 1024, 1024), 1024)
        left = left_ref[:, span]
        for column in range(0, count, 2):
            right = jnp.concatenate([chunk_ref[column, span], chunk_ref[column + 1, span]], axis=1)
            total[:, column * head_dim : (column + 2) * head_dim] += jnp.dot(
                left, right, preferred_element_type=jnp.float32
            )

    out_ref[...] = total[...].astype(jnp.bfloat16)
    for copy in copies:
        copy.wait()


def project(tokens, norm_gain, qkv_weight, places):
    total_rows, pair, local_width = tokens.shape
    groups, columns, head_dim = qkv_weight.shape[1:]
    total_tokens = total_rows * pair
    count = columns // 3
    view = jnp.transpose(qkv_weight, (0, 2, 1, 3))
    vmem = pl.BlockSpec(memory_space=pltpu.VMEM)
    hbm = pl.BlockSpec(memory_space=pl.ANY)
    chunk_shape = jax.ShapeDtypeStruct((count, local_width, groups, head_dim), jnp.bfloat16)
    rows = total_tokens * groups
    params = pltpu.CompilerParams(vmem_limit_bytes=14 << 20)
    left, extra, chunk = pl.pallas_call(
        functools.partial(open_kernel, total_tokens // places, 512),
        out_shape=(
            jax.ShapeDtypeStruct((rows, local_width * groups), jnp.bfloat16),
            jax.ShapeDtypeStruct((rows, head_dim), jnp.bfloat16),
            chunk_shape,
        ),
        in_specs=[vmem, vmem, hbm],
        out_specs=(vmem, vmem, vmem),
        scratch_shapes=[pltpu.SemaphoreType.DMA((count,))],
        compiler_params=params,
    )(tokens.reshape(total_tokens, local_width), norm_gain.reshape(1, local_width), view)
    results = []
    for following in (count, 2 * count, None):
        last = following is None
        out_shape = [jax.ShapeDtypeStruct((rows, count * head_dim), jnp.bfloat16)]
        scratch = [pltpu.VMEM((rows, count * head_dim), jnp.float32)]
        if not last:
            out_shape.append(chunk_shape)
            scratch.append(pltpu.SemaphoreType.DMA((count,)))
        flat = chunk.reshape(count, local_width * groups, head_dim)
        got = pl.pallas_call(
            functools.partial(multiply_kernel, following),
            out_shape=out_shape,
            in_specs=[vmem, vmem, hbm],
            out_specs=[vmem] * len(out_shape),
            scratch_shapes=scratch,
            compiler_params=params,
        )(left, flat, view)
        results.append(got[0])
        if not last:
            chunk = got[1]
    return jnp.concatenate(results + [extra], axis=1)


def body(tokens, norm_gain, qkv_weight, out_weight, kv_cache, lengths, positions):
    rows_local = kv_cache.shape[0]
    head_devices = lax.axis_size("gy")
    width_index = lax.axis_index("gx")
    head_index = lax.axis_index("gy")
    total_rows = tokens.shape[0]
    local_width = tokens.shape[2]
    groups_local = qkv_weight.shape[1]
    group_width = qkv_weight.shape[2]
    head_dim = qkv_weight.shape[3]
    group_size = group_width - 2
    block_rows = rows_local * head_devices
    places = lax.axis_size("gx")
    if groups_local == 2 and group_width % 6 == 0 and local_width % 512 == 0:
        partial_value = project(tokens, norm_gain, qkv_weight, places)
        partial_value = partial_value.reshape(places, groups_local * block_rows * 2, -1)
        pieces = lax.all_to_all(partial_value, "gx", split_axis=0, concat_axis=0)
        summed = jnp.sum(pieces.astype(jnp.float32), axis=0)
        summed = summed.reshape(groups_local, block_rows, 2, group_width + 1, head_dim)
        block_squares = summed[0, :, :, group_width, 0] + summed[0, :, :, group_width, 64]
        block_sum = jnp.transpose(summed[:, :, :, :group_width], (1, 2, 0, 3, 4))
    else:
        tokens_wide = tokens.astype(jnp.float32)
        hidden = (tokens_wide * norm_gain.astype(jnp.float32)).astype(jnp.bfloat16)
        squares = jnp.sum(tokens_wide * tokens_wide, axis=-1)
        partial_value = jnp.dot(
            hidden.reshape(total_rows * 2, local_width),
            qkv_weight.reshape(local_width, -1),
            preferred_element_type=jnp.float32,
        )
        partial_value = partial_value.reshape(total_rows, 2, groups_local, group_width, head_dim)
        block_sum, block_squares = (
            lax.psum_scatter(partial_value, "gx", scatter_dimension=0, tiled=True),
            lax.psum_scatter(squares, "gx", scatter_dimension=0, tiled=True),
        )
    inv_rms = lax.rsqrt(block_squares / D + norm_eps)
    ready = finish(
        block_sum * inv_rms[:, :, None, None, None], positions, width_index * block_rows, block_rows
    )
    packed = lax.all_to_all(ready, "gy", split_axis=0, concat_axis=2, tiled=True)
    queries = packed[:, :, :, :group_size]
    key_new = packed[:, :, :, group_size]
    value_new = packed[:, :, :, group_size + 1]
    attended = attend(queries, key_new, value_new, kv_cache, lengths)
    regrouped = lax.all_to_all(attended, "gy", split_axis=2, concat_axis=0, tiled=True)
    out_flat = out_weight.reshape(-1, local_width)
    row_piece = lax.all_gather(regrouped, "gx", axis=0, tiled=True)
    piece_rows = row_piece.shape[0]
    product = jnp.dot(
        row_piece.reshape(piece_rows * 2, -1), out_flat, preferred_element_type=jnp.float32
    )
    terms = product.astype(jnp.bfloat16).reshape(head_devices, -1, 2, local_width)
    arrived = lax.all_to_all(terms, "gy", split_axis=0, concat_axis=0)
    own_sum = jnp.sum(arrived.astype(jnp.float32), axis=0)
    row_share = total_rows // head_devices
    residual = lax.dynamic_slice_in_dim(tokens, head_index * row_share, row_share, 0).astype(
        jnp.float32
    )
    return residual + own_sum


def solution(mesh):
    return jax.shard_map(
        body,
        mesh=mesh,
        in_specs=(
            P("groups", None, "gx"),
            P("gx"),
            P("gx", "gy", None, None),
            P("gy", None, "gx"),
            P(("groups", "gx", "gy"), None, None, None, None),
            P(("groups", "gx", "gy")),
            P("groups"),
        ),
        out_specs=P(("groups", "gy"), None, "gx"),
        check_vma=False,
    )
```

profile of v0, /device:TPU:0, one launch (start us, length us, event | category | flops | bytes accessed | tf_op | source)
XLA Modules:
  0.0 101.6 jit_solution(7988507802875561067)
XLA Ops:
  0.0 1.2 %reshape.125.tokens_ref = bf16[64,4096]{1,0:T(8,128)(2,1)S(1)} reshape(bf16[32,2,4096]{2,1,0:T(2,128)(2,1)} %param.7) | data formatting | bytes 1048576 | tf_op jit(solution)/shard_map/reshape | solution.py:182
  1.2 0.7 reshape.126.gain_ref
  2.0 4.8 %shard_map.73 = (bf16[128,8192]{1,0:T(8,128)(2,1)S(1)}, bf16[128,128]{1,0:T(8,128)(2,1)S(1)}, bf16[6,4096,2,128]{3,2,1,0:T(2,128)(2,1)S(1)}) custom-call(bf16[64,4096]{1,0:T(8,128)(2,1)S(1)} %reshape.125.tokens_ref, bf16[1,4096]{1,0:T(2,128)(2,1)S(1)} %reshape.126.gain_ref, bf16[4096,18,2,128]{3,2,1,0:T(2,128)(2,1)} %bitcast.73), custom_call_target="tpu_custom_call" | custom-call | tf_op jit(solution)/shard_map/pallas_call | solution.py:171
  6.8 4.8 %shard_map.74 = (bf16[128,768]{1,0:T(8,128)(2,1)S(1)}, bf16[6,4096,2,128]{3,2,1,0:T(2,128)(2,1)S(1)}) custom-call(bf16[128,8192]{1,0:T(8,128)(2,1)S(1)} %get-tuple-element.12.left_ref, bf16[6,8192,128]{2,1,0:T(8,128)(2,1)S(1)} %bitcast.70, bf16[4096,18,2,128]{3,2,1,0:T(2,128)(2,1)} %bitcast.74), custom_call_target="tpu_custom_call" | custom-call | tf_op jit(solution)/shard_map/pallas_call | solution.py:192
  11.6 4.8 %shard_map.75 = (bf16[128,768]{1,0:T(8,128)(2,1)S(1)}, bf16[6,4096,2,128]{3,2,1,0:T(2,128)(2,1)S(1)}) custom-call(bf16[128,8192]{1,0:T(8,128)(2,1)S(1)} %get-tuple-element.12.left_ref, bf16[6,8192,128]{2,1,0:T(8,128)(2,1)S(1)} %bitcast.71, bf16[4096,18,2,128]{3,2,1,0:T(2,128)(2,1)} %bitcast.75), custom_call_target="tpu_custom_call" | custom-call | tf_op jit(solution)/shard_map/pallas_call | solution.py:192
  16.4 3.1 %shard_map.76 = bf16[128,768]{1,0:T(8,128)(2,1)S(1)} custom-call(bf16[128,8192]{1,0:T(8,128)(2,1)S(1)} %get-tuple-element.12.left_ref, bf16[6,8192,128]{2,1,0:T(8,128)(2,1)S(1)} %bitcast.72, bf16[4096,18,2,128]{3,2,1,0:T(2,128)(2,1)} %bitcast.76), custom_call_target="tpu_custom_call" | custom-call | tf_op jit(solution)/shard_map/pallas_call | solution.py:192
  19.5 0.0 copy-start.2
  19.5 0.9 pad_maximum_fusion
  20.4 4.3 %all-to-all-start = ((bf16[4,32,2432]{2,1,0:T(8,128)(2,1)}), bf16[4,32,2432]{2,1,0:T(8,128)(2,1)S(1)}, u32[]{:S(2)}, u32[]{:S(2)}) async-start(bf16[4,32,2432]{2,1,0:T(8,128)(2,1)} %bitcast.4), calls=%async_computation | async-start | bytes 1245184 | tf_op jit(solution)/shard_map/all_to_all | solution.py:222
  24.6 0.0 copy-done.2
  24.6 0.1 dynamic_slice.7
  24.7 0.1 add_convert_fusion.2
  24.8 0.2 multiply_cosine_fusion
  25.0 3.3 %fusion.21 = (bf16[2,384,1,8,128]{4,3,2,1,0:T(8,128)(2,1)}, bf16[2,384,1,8,128]{4,3,2,1,0:T(8,128)(2,1)S(1)}) fusion(bf16[2,384,2,8,128]{4,3,2,1,0:T(8,128)(2,1)} %param.11), kind=kLoop, calls=%fused_computation.50 | loop fusion | bytes 6291456 | tf_op jit(solution)/shard_map/slice | solution.py:68
  28.3 6.2 %all-to-all-done = bf16[4,32,2432]{2,1,0:T(8,128)(2,1)S(1)} async-done(((bf16[4,32,2432]{2,1,0:T(8,128)(2,1)}), bf16[4,32,2432]{2,1,0:T(8,128)(2,1)S(1)}, u32[]{:S(2)}, u32[]{:S(2)}) %all-to-all-start) | async-done | bytes 622624 | tf_op jit(solution)/shard_map/all_to_all | solution.py:222
  34.5 0.1 convert_reduce_fusion
  34.6 0.0 copy-start.1
  34.6 0.1 fusion.22
  34.7 0.1 copy.72
  34.8 0.1 copy.73
  34.9 0.1 copy.50
  35.0 0.1 fusion.11
  35.1 0.1 subtract_convert_fusion.1
  35.3 0.2 subtract_convert_fusion
  35.4 0.1 pad_maximum_fusion.1
  35.6 0.8 copy.51
  36.4 5.5 %all-to-all-start.1 = ((bf16[8,2,2,18,128]{4,2,3,1,0:T(2,128)(2,1)}), bf16[8,2,2,18,128]{4,2,3,1,0:T(2,128)(2,1)S(1)}, u32[]{:S(2)}, u32[]{:S(2)}) async-start(bf16[8,2,2,18,128]{4,2,3,1,0:T(2,128)(2,1)} %copy.51), calls=%async_computation.1 | async-start | bytes 294912 | tf_op jit(solution)/shard_map/all_to_all | solution.py:245
  41.9 0.0 copy-done.1
  41.9 0.1 iota_compare_fusion
  42.0 6.2 %all-to-all-done.1 = bf16[8,2,2,18,128]{4,2,3,1,0:T(2,128)(2,1)S(1)} async-done(((bf16[8,2,2,18,128]{4,2,3,1,0:T(2,128)(2,1)}), bf16[8,2,2,18,128]{4,2,3,1,0:T(2,128)(2,1)S(1)}, u32[]{:S(2)}, u32[]{:S(2)}) %all-to-all-start.1) | async-done | bytes 147488 | tf_op jit(solution)/shard_map/all_to_all | solution.py:245
  48.3 0.4 fusion.25
  48.7 0.0 copy-start
  48.7 0.8 fusion.24
  49.5 0.3 fusion.10
  49.8 0.1 fusion.16
  49.9 0.2 convolution_bitcast_fusion
  50.2 0.0 copy-done
  50.2 0.5 fusion.7
  50.7 8.3 %all_to_all.46 = bf16[2,2,8,16,128]{4,3,1,0,2:T(8,128)(2,1)S(1)} all-to-all(bf16[2,2,8,16,128]{4,3,1,0,2:T(8,128)(2,1)S(1)} %copy.60), channel_id=1, replica_groups=mesh['groups'=2,'gx'=4,'gy'=4] {'gy'}, dimensions={2} | all-to-all | bytes 262144 | tf_op jit(solution)/shard_map/all_to_all | solution.py:250
  59.1 6.5 %all_gather.3 = bf16[32,2,2,16,128]{4,3,2,1,0:T(8,128)(2,1)S(1)} all-gather(bf16[8,2,2,16,128]{4,3,2,1,0:T(8,128)(2,1)S(1)} %bitcast.82), channel_id=1, replica_groups=mesh['groups'=2,'gx'=4,'gy'=4] {'gx'}, dimensions={0}, use_global_device_ids=true | all-gather | bytes 655360 | tf_op jit(solution)/shard_map/all_gather | solution.py:252
  65.6 0.2 reshape.132
  65.8 13.6 %convolution_convert_fusion = bf16[64,4096]{1,0:T(8,128)(2,1)S(1)} fusion(bf16[64,4096]{1,0:T(8,128)(2,1)S(1)} %reshape.132, bf16[4096,4096]{1,0:T(8,128)(2,1)} %bitcast.77), kind=kOutput, calls=%fused_computation | convolution fusion | flops 2147745792 | bytes 34603008 | tf_op jit(solution)/shard_map/dot_general | solution.py:254
  79.5 1.1 %reshape.134 = bf16[4,8,2,4096]{3,2,1,0:T(2,128)(2,1)} reshape(bf16[64,4096]{1,0:T(8,128)(2,1)S(1)} %convolution_convert_fusion) | data formatting | bytes 1048576 | tf_op jit(solution)/shard_map/reshape | solution.py:257
  80.6 3.5 %all-to-all-start.3 = ((bf16[4,8,2,4096]{3,2,1,0:T(2,128)(2,1)}), bf16[4,8,2,4096]{3,2,1,0:T(2,128)(2,1)S(1)}, u32[]{:S(2)}, u32[]{:S(2)}) async-start(bf16[4,8,2,4096]{3,2,1,0:T(2,128)(2,1)} %reshape.134), calls=%async_computation.3 | async-start | bytes 1048576 | tf_op jit(solution)/shard_map/all_to_all | solution.py:258
  84.1 15.2 %all-to-all-done.3 = bf16[4,8,2,4096]{3,2,1,0:T(2,128)(2,1)S(1)} async-done(((bf16[4,8,2,4096]{3,2,1,0:T(2,128)(2,1)}), bf16[4,8,2,4096]{3,2,1,0:T(2,128)(2,1)S(1)}, u32[]{:S(2)}, u32[]{:S(2)}) %all-to-all-start.3) | async-done | bytes 524320 | tf_op jit(solution)/shard_map/all_to_all | solution.py:258
  99.3 0.6 convert_reduce_fusion.1
  99.9 1.8 %convert_add_fusion = f32[8,2,4096]{2,1,0:T(2,128)} fusion(f32[8,2,4096]{2,1,0:T(2,128)S(1)} %convert_reduce_fusion.1, bf16[32,2,4096]{2,1,0:T(2,128)(2,1)} %param.7, s32[]{:T(128)S(6)} %select_n.17), kind=kLoop, calls=%fused_computation.27 | loop fusion | flops 131072 | bytes 655364 | tf_op jit(solution)/shard_map/add | solution.py:264
  (13 shorter events, 0.2 us)
Async XLA Ops:
  19.5 5.2 %copy-start.2 = (s32[32]{0:T(128)S(1)}, s32[32]{0:T(128)}, u32[]{:S(2)}) copy-start(s32[32]{0:T(128)} %param.13) | copy-start | bytes 388
  20.4 14.1 %all-to-all-start = ((bf16[4,32,2432]{2,1,0:T(8,128)(2,1)}), bf16[4,32,2432]{2,1,0:T(8,128)(2,1)S(1)}, u32[]{:S(2)}, u32[]{:S(2)}) async-start(bf16[4,32,2432]{2,1,0:T(8,128)(2,1)} %bitcast.4), calls=%async_computation | async-start | bytes 1245184 | tf_op jit(solution)/shard_map/all_to_all | solution.py:222
  34.6 7.3 %copy-start.1 = (s32[2]{0:T(128)S(1)}, s32[2]{0:T(128)}, u32[]{:S(2)}) copy-start(s32[2]{0:T(128)} %param.12) | copy-start | bytes 28
  36.4 11.8 %all-to-all-start.1 = ((bf16[8,2,2,18,128]{4,2,3,1,0:T(2,128)(2,1)}), bf16[8,2,2,18,128]{4,2,3,1,0:T(2,128)(2,1)S(1)}, u32[]{:S(2)}, u32[]{:S(2)}) async-start(bf16[8,2,2,18,128]{4,2,3,1,0:T(2,128)(2,1)} %copy.51), calls=%async_computation.1 | async-start | bytes 294912 | tf_op jit(solution)/shard_map/all_to_all | solution.py:245
  48.7 1.5 %copy-start = (bf16[2,384,1,8,128]{4,3,2,1,0:T(8,128)(2,1)S(1)}, bf16[2,384,1,8,128]{4,3,2,1,0:T(8,128)(2,1)}, u32[]{:S(2)}) copy-start(bf16[2,384,1,8,128]{4,3,2,1,0:T(8,128)(2,1)} %get-tuple-element.19) | copy-start | bytes 4718596
  80.6 18.7 %all-to-all-start.3 = ((bf16[4,8,2,4096]{3,2,1,0:T(2,128)(2,1)}), bf16[4,8,2,4096]{3,2,1,0:T(2,128)(2,1)S(1)}, u32[]{:S(2)}, u32[]{:S(2)}) async-start(bf16[4,8,2,4096]{3,2,1,0:T(2,128)(2,1)} %reshape.134), calls=%async_computation.3 | async-start | bytes 1048576 | tf_op jit(solution)/shard_map/all_to_all | solution.py:258
where the time goes:
time: 102 us
  waiting for transfers between devices  27.6 us (27%)
  Pallas kernels  17.5 us (17%)
  matrix products  15.6 us (15%)
  blocking collectives  14.8 us (15%)
  starting transfers between devices  13.3 us (13%)
  local copies, waits for them, and re-layouts  7.99 us (8%)
  other arithmetic  4.58 us (4%)
    all_to_all x1, waiting for transfers between devices, body(): arrived = lax.all_to_all(terms, 'gy', split_axis=0, concat_axis=0)  15.2 us
    dot_general x1, matrix products, body(): jnp.dot(row_piece.reshape(piece_rows * 2, -1), out_flat, preferred_elemen...  13.6 us
    pallas_call x3, Pallas kernels, project(): pl.pallas_call(functools.partial(multiply_kernel, following), out_shape=o...  12.7 us
    all_to_all x1, blocking collectives, body(): lax.all_to_all(attended, 'gy', split_axis=2, concat_axis=0, tiled=True)  8.34 us
    all_gather x1, blocking collectives, body(): row_piece = lax.all_gather(regrouped, 'gx', axis=0, tiled=True)  6.5 us
    all_to_all x1, waiting for transfers between devices, body(): pieces = lax.all_to_all(partial_value, 'gx', split_axis=0, concat_axis=0)  6.22 us
    all_to_all x1, waiting for transfers between devices, body(): lax.all_to_all(ready, 'gy', split_axis=0, concat_axis=2, tiled=True)  6.15 us
    all_to_all x1, starting transfers between devices, body(): lax.all_to_all(ready, 'gy', split_axis=0, concat_axis=2, tiled=True)  5.53 us
  transfers between devices with their start and end apart: 3, of which 3 were waited for; matrix products, arithmetic and copies ran while one was open for 4% of the time, Pallas kernels for 0%

commit v1 on v0

v1 whole, which is shorter than its diff:
```python
import functools
import math

import jax
import jax.numpy as jnp
from jax import lax
from jax.experimental import pallas as pl
from jax.experimental.pallas import tpu as pltpu
from jax.sharding import PartitionSpec as P

D = 16384


norm_eps = 1e-05
rope_base = 500000.0


def rotate(values, places):
    half_dim = values.shape[-1] // 2
    index_half = jnp.arange(half_dim, dtype=jnp.float32)
    frequency = rope_base ** (-2.0 * index_half / values.shape[-1])
    angles = places[..., None] * frequency
    cosine = jnp.cos(angles)
    sine_part = jnp.sin(angles)
    front_half = values[..., :half_dim]
    back_half = values[..., half_dim:]
    return jnp.concatenate(
        [front_half * cosine - back_half * sine_part, back_half * cosine + front_half * sine_part],
        axis=-1,
    )


def finish(projected, positions, first_row, row_count):
    group_size = projected.shape[3] - 2
    placed = lax.dynamic_slice_in_dim(positions, first_row, row_count, 0)
    places = (placed[:, None] + jnp.arange(2, dtype=jnp.int32)[None, :]).astype(jnp.float32)
    queries = rotate(projected[:, :, :, :group_size], places[:, :, None, None])
    key_new = rotate(projected[:, :, :, group_size : group_size + 1], places[:, :, None, None])
    value_new = projected[:, :, :, group_size + 1 :]
    return jnp.concatenate([queries, key_new, value_new], axis=3).astype(jnp.bfloat16)


def attend(queries, key_new, value_new, cache_rows, length):
    scale_factor = 1.0 / math.sqrt(queries.shape[-1])
    scores_old = (
        jnp.einsum(
            "rtgid,rsgd->rtgis", queries, cache_rows[:, :, 0], preferred_element_type=jnp.float32
        )
        * scale_factor
    )
    slot_ids = jnp.arange(cache_rows.shape[1], dtype=jnp.int32)
    visible = slot_ids[None, :] < length[:, None]
    scores_old = jnp.where(visible[:, None, None, None, :], scores_old, -1e30)
    scores_new = (
        jnp.einsum("rtgid,rugd->rtgiu", queries, key_new, preferred_element_type=jnp.float32)
        * scale_factor
    )
    token_ids = jnp.arange(queries.shape[1], dtype=jnp.int32)
    causal = token_ids[:, None] >= token_ids[None, :]
    scores_new = jnp.where(causal[None, :, None, None, :], scores_new, -1e30)
    highest = jnp.maximum(jnp.max(scores_old, axis=-1), jnp.max(scores_new, axis=-1))
    expo_old = jnp.exp(scores_old - highest[..., None])
    expo_new = jnp.exp(scores_new - highest[..., None])
    denominator = jnp.sum(expo_old, axis=-1) + jnp.sum(expo_new, axis=-1)
    weight_old = (expo_old / denominator[..., None]).astype(jnp.bfloat16)
    weight_new = (expo_new / denominator[..., None]).astype(jnp.bfloat16)
    attended = jnp.einsum(
        "rtgis,rsgd->rtgid", weight_old, cache_rows[:, :, 1], preferred_element_type=jnp.float32
    )
    attended = attended + jnp.einsum(
        "rtgiu,rugd->rtgid", weight_new, value_new, preferred_element_type=jnp.float32
    )
    return attended.astype(jnp.bfloat16)


def hop(source, target, sends, arrivals, place):
    return pltpu.make_async_remote_copy(
        src_ref=source,
        dst_ref=target,
        send_sem=sends,
        recv_sem=arrivals,
        device_id=place,
        device_id_type=pl.DeviceIdType.MESH,
    )


def block_kernel(
    head_devices,
    places,
    tokens_ref,
    gain_ref,
    qkv_ref,
    out_weight_ref,
    cache_ref,
    lengths_ref,
    positions_ref,
    out_ref,
    raw,
    tok,
    gain,
    gain_wide,
    left,
    ring,
    chunk,
    weights,
    own_sum,
    core_send,
    core_recv,
    row_send,
    row_recv,
    square_all,
    square_core,
    square_mid,
    square_recv,
    query_buf,
    attended_buf,
    attended_send,
    attended_recv,
    part_send,
    part_recv,
    part_own,
    load_sems,
    ring_sems,
    tile_sems,
    weight_sems,
    core_sems,
    row_sends,
    row_recvs,
    square_sems,
    att_sends,
    att_recvs,
    pair_sends,
    pair_recvs,
    part_sends,
    part_recvs,
):
    f32, bf16 = jnp.float32, jnp.bfloat16
    rows_total, pair, local_width = raw.shape
    total_tokens = rows_total * pair
    columns, head_dim = qkv_ref.shape[1], qkv_ref.shape[3]
    groups = qkv_ref.shape[2]
    group_size = columns - 2
    pieces = columns // 2
    slots = ring.shape[0]
    max_len = (cache_ref.shape[0] // (2 * groups * head_devices)) // lengths_ref.shape[0]
    rows_local = lengths_ref.shape[0]
    all_groups = groups * head_devices
    near = rows_local * pair
    block = groups * near
    lanes = places // 2
    team = lanes * head_devices
    contraction = local_width * groups
    width = lax.axis_index("gx")
    head = lax.axis_index("gy")
    core = lax.rem(width, 2)
    lane_at = width // 2
    mine = lane_at * head_devices + head
    source_at = width * head_devices + head
    partner = {"gx": width + 1 - 2 * core}

    def member(off):
        other = lax.rem(mine + off, team)
        far_lane, far_head = other // head_devices, lax.rem(other, head_devices)
        return other, {"gx": far_lane * 2 + core, "gy": far_head}

    def bring(piece, slot):
        return [
            pltpu.make_async_copy(
                qkv_ref.at[:, piece * 2 + at], ring.at[slot, at], ring_sems.at[slot, at]
            )
            for at in range(2)
        ]

    load_tokens = pltpu.make_async_copy(tokens_ref, raw, load_sems.at[0])
    load_gain = pltpu.make_async_copy(gain_ref, gain, load_sems.at[1])
    load_tokens.start()
    load_gain.start()
    for piece in range(min(slots, pieces)):
        for copy in bring(piece, piece):
            copy.start()
    barrier = pltpu.get_barrier_semaphore()
    pl.semaphore_signal(barrier, inc=1, device_id=partner, device_id_type=pl.DeviceIdType.MESH)
    for off in range(1, team):
        pl.semaphore_signal(
            barrier, inc=1, device_id=member(off)[1], device_id_type=pl.DeviceIdType.MESH
        )

    made = lax.broadcasted_iota(jnp.int32, (total_tokens * groups, total_tokens), 0)
    held = lax.broadcasted_iota(jnp.int32, (total_tokens * groups, total_tokens), 1)
    target = made // block
    owner_core = target // team
    owner_lane = lax.rem(target, team) // head_devices
    owner_head = lax.rem(target, head_devices)
    owner = (owner_lane * 2 + owner_core) * head_devices + owner_head
    chosen = owner * near + lax.rem(made, near) == held
    chooser = jnp.where(chosen, 1.0, 0.0)
    group_row = lax.rem(
        lax.broadcasted_iota(jnp.int32, (total_tokens * groups, 128), 0), block
    ) // near
    feature = lax.broadcasted_iota(jnp.int32, (128 * groups, 128 * groups), 0)
    goal = lax.broadcasted_iota(jnp.int32, (128 * groups, 128 * groups), 1)
    spread = jnp.where(
        goal == lax.rem(feature, 128) * groups + feature // 128, 1.0, 0.0
    ).astype(bf16)

    load_tokens.wait()
    retile = pltpu.make_async_copy(
        raw.reshape(total_tokens, local_width), tok, load_sems.at[2]
    )
    retile.start()
    load_gain.wait()
    gain_wide[...] = gain[...].astype(f32)
    retile.wait()
    depth = 512

    def widen(at, squares):
        start = pl.multiple_of(at * depth, depth)
        wide = tok[:, pl.ds(start, depth)].astype(f32)
        scale = jnp.concatenate(
            [gain_wide[pl.ds(at * (depth // 128) + q, 1), :] for q in range(depth // 128)], axis=1
        )
        hidden = (wide * scale).astype(bf16)
        ordered = jnp.dot(chooser.astype(bf16), hidden, preferred_element_type=f32)
        for q in range(depth // 128):
            part = wide[:, q * 128 : (q + 1) * 128]
            squares += part * part
            near_part = ordered[:, q * 128 : (q + 1) * 128]
            split = jnp.concatenate(
                [jnp.where(group_row == group, near_part, 0.0) for group in range(groups)], axis=1
            ).astype(bf16)
            begin = pl.multiple_of((start + q * 128) * groups, 128 * groups)
            left[:, pl.ds(begin, 128 * groups)] = jnp.dot(
                split, spread, preferred_element_type=f32
            ).astype(bf16)
        return squares

    squares = lax.fori_loop(
        0, local_width // depth, widen, jnp.zeros((total_tokens, 128), f32)
    )
    square_all[...] = jnp.dot(
        chooser, squares, preferred_element_type=f32, precision=lax.Precision.HIGHEST
    ).reshape(square_all.shape)
    pl.semaphore_wait(barrier, team)

    square_hop = hop(
        square_all.at[1 - core], square_core, square_sems.at[0], square_sems.at[1], partner
    )
    square_hop.start()

    def core_hop(piece):
        return hop(
            core_send.at[piece],
            core_recv.at[piece],
            core_sems.at[0, piece],
            core_sems.at[1, piece],
            partner,
        )

    def row_hop(piece, off):
        other, place = member(off)
        return hop(
            row_send.at[piece, other],
            row_recv.at[piece, mine],
            row_sends.at[piece, other],
            row_recvs.at[piece, mine],
            place,
        )

    def row_arrival(piece, off):
        other, place = member(off)
        return hop(
            row_send.at[piece, other],
            row_recv.at[piece, other],
            row_sends.at[piece, other],
            row_recvs.at[piece, other],
            place,
        )

    def pass_on(piece):
        core_hop(piece).wait_recv()
        total = own_sum[lax.rem(piece, 2), core] + core_recv[piece].astype(f32)
        row_send[piece] = total.reshape(row_send.shape[1:]).astype(bf16)
        row_recv[piece, mine] = row_send[piece, mine]
        for off in range(1, team):
            row_hop(piece, off).start()

    def weight_copy(at):
        across = part_own.shape[2]
        return pltpu.make_async_copy(
            out_weight_ref.at[:, pl.ds(at * across, across)],
            weights.at[:, pl.ds(at * across, across)],
            weight_sems.at[at],
        )

    stretches = part_own.shape[0]
    cache_slot, cached_slot = pieces % 2, (pieces - 1) % 2
    cache_rows = cache_ref.shape[0]
    load_cache = pltpu.make_async_copy(
        cache_ref, chunk.at[cache_slot, pl.ds(0, cache_rows)], load_sems.at[3]
    )

    @pl.loop(0, pieces)
    def _(piece):
        slot, here = lax.rem(piece, slots), lax.rem(piece, 2)
        for copy in bring(piece, slot):
            copy.wait()
        flat = ring.reshape(slots, 2, contraction, head_dim)
        moves = [
            pltpu.make_async_copy(
                flat.at[slot, at],
                chunk.at[here, pl.ds(at * contraction, contraction)],
                tile_sems.at[at],
            )
            for at in range(2)
        ]
        for move in moves:
            move.start()

        @pl.when(piece == pieces - 1)
        def _():
            load_cache.start()
            for at in range(stretches):
                weight_copy(at).start()

        for move in moves:
            move.wait()

        @pl.when(piece + slots < pieces)
        def _():
            for copy in bring(piece + slots, slot):
                copy.start()

        right = jnp.concatenate(
            [chunk[here, pl.ds(0, contraction)], chunk[here, pl.ds(contraction, contraction)]], axis=1
        )
        total = jnp.dot(left[...], right, preferred_element_type=f32)
        own_sum[here] = total.reshape(own_sum.shape[1:])
        core_send[piece] = own_sum[here, 1 - core].astype(bf16)
        core_hop(piece).start()

        @pl.when(piece >= 1)
        def _():
            pass_on(piece - 1)

    pass_on(pieces - 1)
    square_hop.wait_recv()
    square_mid[...] = (square_all[core] + square_core[...]).reshape(square_mid.shape)
    square_recv[lane_at] = square_mid[mine]

    def square_send(off):
        other_lane = lax.rem(lane_at + off, lanes)
        return hop(
            square_mid.at[other_lane * head_devices + head],
            square_recv.at[lane_at],
            square_sems.at[2 + 2 * off],
            square_sems.at[3 + 2 * off],
            {"gx": other_lane * 2 + core},
        )

    def square_arrival(off):
        other_lane = lax.rem(lane_at + lanes - off, lanes)
        return hop(
            square_mid.at[mine],
            square_recv.at[other_lane],
            square_sems.at[2 + 2 * off],
            square_sems.at[3 + 2 * off],
            {"gx": other_lane * 2 + core},
        )

    for off in range(1, lanes):
        square_send(off).start()

    stride = max_len + 16
    steps = 16
    kinds = 2 * all_groups
    size = steps * kinds
    to_row = lax.broadcasted_iota(jnp.int32, (size, size), 0)
    from_row = lax.broadcasted_iota(jnp.int32, (size, size), 1)
    regroup = jnp.where(
        from_row == lax.rem(to_row, steps) * kinds + to_row // steps, 1.0, 0.0
    ).astype(bf16)
    load_cache.wait()
    for row in range(rows_local):

        @pl.loop(0, max_len // (2 * steps))
        def _(step):
            first = pl.multiple_of(row * max_len * kinds + step * 2 * size, size)
            both = jnp.concatenate(
                [chunk[cache_slot, pl.ds(first, size)], chunk[cache_slot, pl.ds(first + size, size)]],
                axis=1,
            )
            sorted_rows = jnp.dot(regroup, both, preferred_element_type=f32).astype(bf16)
            for kind in range(kinds):
                base = (row * kinds + kind) * stride
                for half in range(2):
                    at = pl.multiple_of(base + (step * 2 + half) * steps, 16)
                    chunk[cached_slot, pl.ds(at, steps)] = sorted_rows[
                        kind * steps : (kind + 1) * steps, half * head_dim : (half + 1) * head_dim
                    ]

    row_at = lax.broadcasted_iota(jnp.int32, (block, head_dim), 0)
    lane = lax.broadcasted_iota(jnp.int32, (block, head_dim), 1)
    half_dim = head_dim // 2
    place = jnp.zeros((block, head_dim), jnp.int32)
    for row in range(rows_local):
        place = jnp.where(
            lax.rem(row_at, near) // pair == row, positions_ref[source_at * rows_local + row], place
        )
    place = (place + lax.rem(row_at, pair)).astype(f32)
    index_half = lax.rem(lane, half_dim).astype(f32)
    frequency = jnp.exp(index_half * (-2.0 * math.log(rope_base) / head_dim))
    angles = place * frequency
    cosine = jnp.cos(angles)
    sine = jnp.where(lane < half_dim, -jnp.sin(angles), jnp.sin(angles))

    for off in range(1, lanes):
        square_arrival(off).wait_recv()
    square_total = square_recv[0]
    for at in range(1, lanes):
        square_total = square_total + square_recv[at]
    inv_rms = lax.rsqrt(
        jnp.sum(square_total, axis=1, keepdims=True) / (local_width * places) + norm_eps
    )

    @pl.loop(0, pieces)
    def _(piece):
        for off in range(1, team):
            row_arrival(piece, off).wait_recv()

    small = lax.broadcasted_iota(jnp.int32, (block, head_dim), 0)
    for far in range(head_devices):
        for column in range(columns):
            piece, side = column // 2, column % 2
            value = row_recv[piece, far, :, side * head_dim : (side + 1) * head_dim].astype(f32)
            for at in range(1, lanes):
                value = value + row_recv[
                    piece, at * head_devices + far, :, side * head_dim : (side + 1) * head_dim
                ].astype(f32)
            value = value * inv_rms
            if column <= group_size:
                turned = jnp.concatenate([value[:, half_dim:], value[:, :half_dim]], axis=1)
                value = value * cosine + turned * sine
            if column < group_size:
                query_buf[far, column * block : (column + 1) * block, :] = value
            else:
                kind = column - group_size
                for group in range(groups):
                    for row in range(rows_local):
                        start = group * near + row * pair
                        moved = pltpu.roll(value, (block - start) % block, 0) if start else value
                        fresh = jnp.where(small < pair, moved, 0.0)
                        base = (
                            row * kinds + kind * all_groups + far * groups + group
                        ) * stride + max_len
                        chunk[cached_slot, pl.ds(base, 16)] = jnp.concatenate(
                            [fresh, jnp.zeros((16 - block, head_dim), f32)], axis=0
                        ).astype(bf16)

    scale_factor = 1.0 / math.sqrt(head_dim)
    count = pair * group_size
    slot_id = lax.broadcasted_iota(jnp.int32, (count, stride), 1)
    token_id = lax.broadcasted_iota(jnp.int32, (count, stride), 0) // group_size
    fresh_seen = (slot_id >= max_len) & (slot_id - max_len <= token_id)
    for row in range(rows_local):
        seen = (slot_id < lengths_ref[row]) | fresh_seen
        for every in range(all_groups):
            far, group = every // groups, every % groups
            first = group * near + row * pair
            queries = jnp.concatenate(
                [
                    query_buf[far, pl.ds(first + token, group_size, stride=block), :]
                    for token in range(pair)
                ],
                axis=0,
            ).astype(bf16)
            keys = chunk[cached_slot, pl.ds((row * kinds + every) * stride, stride)]
            values = chunk[cached_slot, pl.ds((row * kinds + all_groups + every) * stride, stride)]
            scores = lax.dot_general(
                queries, keys, (((1,), (1,)), ((), ())), preferred_element_type=f32
            )
            scores = jnp.where(seen, scores * scale_factor, -1e30)
            expo = jnp.exp(scores - jnp.max(scores, axis=1, keepdims=True))
            weight = (expo / jnp.sum(expo, axis=1, keepdims=True)).astype(bf16)
            result = jnp.dot(weight, values, preferred_element_type=f32)
            for token in range(pair):
                attended_buf[far, pl.ds(first + token, group_size, stride=block), :] = result[
                    token * group_size : (token + 1) * group_size
                ]
    for far in range(head_devices):
        for at in range(group_size):
            attended_send[far, :, at * head_dim : (at + 1) * head_dim] = attended_buf[
                far, at * block : (at + 1) * block, :
            ].astype(bf16)

    def att_hop(off):
        other, place_of = member(off)
        return hop(
            attended_send.at[place_of["gy"]],
            attended_recv.at[source_at],
            att_sends.at[other],
            att_recvs.at[mine],
            place_of,
        )

    def source_of(other, which):
        return ((other // head_devices) * 2 + which) * head_devices + lax.rem(other, head_devices)

    def att_arrival(off):
        other, place_of = member(off)
        return hop(
            attended_send.at[place_of["gy"]],
            attended_recv.at[source_of(other, core)],
            att_sends.at[other],
            att_recvs.at[other],
            place_of,
        )

    def pair_hop(other, which):
        from_at = source_of(other, which)
        return hop(
            attended_recv.at[from_at],
            attended_recv.at[from_at],
            pair_sends.at[other],
            pair_recvs.at[other],
            partner,
        )

    for off in range(team - 1, 0, -1):
        att_hop(off).start()
    attended_recv[source_at] = attended_send[head]
    pair_hop(mine, core).start()
    for off in range(1, team):
        att_arrival(off).wait_recv()
        pair_hop(lax.rem(mine + off, team), core).start()
    for off in range(team):
        pair_hop(lax.rem(mine + off, team), 1 - core).wait_recv()

    heads_width = group_size * head_dim
    sources = places * head_devices
    first_rows = lax.rem(lax.broadcasted_iota(jnp.int32, (2 * block, heads_width), 0), block) // near
    for at in range(0, sources, 2):
        both = jnp.concatenate([attended_recv[at], attended_recv[at + 1]], axis=0).astype(f32)
        for group in range(groups):
            left[at * block : (at + 2) * block, group * heads_width : (group + 1) * heads_width] = (
                jnp.where(first_rows == group, both, 0.0).astype(bf16)
            )

    def part_hop(at, off):
        other = lax.rem(head + off, head_devices)
        return hop(
            part_send.at[at, other],
            part_recv.at[at, head],
            part_sends.at[at, other],
            part_recvs.at[at, head],
            {"gy": other},
        )

    def part_arrival(at, off):
        other = lax.rem(head + off, head_devices)
        return hop(
            part_send.at[at, other],
            part_recv.at[at, other],
            part_sends.at[at, other],
            part_recvs.at[at, other],
            {"gy": other},
        )

    across = part_own.shape[2]
    share = total_tokens // head_devices

    @pl.loop(0, stretches)
    def _(at):
        weight_copy(at).wait()
        span = pl.ds(pl.multiple_of(at * across, across), across)
        product = jnp.dot(
            left[:, : groups * heads_width], weights[:, span], preferred_element_type=f32
        )
        upper = lax.broadcasted_iota(jnp.int32, (block, across), 0) < near
        tiles = []
        for source in range(sources):
            tile = product[source * block : (source + 1) * block]
            tiles.append(tile + pltpu.roll(tile, near, 0))
        joined = [
            jnp.where(upper, tiles[source], tiles[source + 1]) for source in range(0, sources, 2)
        ]
        per = len(joined) // head_devices
        for far in range(head_devices):
            value = jnp.concatenate(joined[far * per : (far + 1) * per], axis=0)
            part_send[at, far] = value.astype(bf16)

            @pl.when(far == head)
            def _():
                part_own[at] = value

        for off in range(1, head_devices):
            part_hop(at, off).start()

    mine_rows = pl.ds(pl.multiple_of(head * share, share), share)

    @pl.loop(0, stretches)
    def _(at):
        span = pl.ds(pl.multiple_of(at * across, across), across)
        value = part_own[at] + tok[mine_rows, span].astype(f32)
        for off in range(1, head_devices):
            part_arrival(at, off).wait_recv()
            value = value + part_recv[at, lax.rem(head + off, head_devices)].astype(f32)
        out_ref[:, span] = value

    square_hop.wait_send()
    for off in range(1, lanes):
        square_send(off).wait_send()

    @pl.loop(0, pieces)
    def _(piece):
        core_hop(piece).wait_send()
        for off in range(1, team):
            row_hop(piece, off).wait_send()

    for off in range(1, team):
        att_hop(off).wait_send()
    for off in range(team):
        pair_hop(lax.rem(mine + off, team), core).wait_send()

    @pl.loop(0, stretches)
    def _(at):
        for off in range(1, head_devices):
            part_hop(at, off).wait_send()


def whole_block(tokens, norm_gain, qkv_weight, out_weight, kv_cache, lengths, positions):
    f32, bf16 = jnp.float32, jnp.bfloat16
    rows_total, pair, local_width = tokens.shape
    groups, columns, head_dim = qkv_weight.shape[1:]
    places, head_devices = lax.axis_size("gx"), lax.axis_size("gy")
    rows_local, max_len = kv_cache.shape[:2]
    total_tokens = rows_total * pair
    group_size = columns - 2
    pieces = columns // 2
    slots = 3
    lanes = places // 2
    team = lanes * head_devices
    block = groups * rows_local * pair
    sources = places * head_devices
    share = total_tokens // head_devices
    across = 512
    stretches = local_width // across
    contraction = local_width * groups
    wide = 2 * head_dim
    hbm = pl.BlockSpec(memory_space=pl.ANY)
    smem = pl.BlockSpec(memory_space=pltpu.SMEM)
    dma = pltpu.SemaphoreType.DMA
    got = pl.pallas_call(
        functools.partial(block_kernel, head_devices, places),
        out_shape=jax.ShapeDtypeStruct((share, local_width), f32),
        in_specs=[hbm, hbm, hbm, hbm, hbm, smem, smem],
        out_specs=pl.BlockSpec(memory_space=pltpu.VMEM),
        scratch_shapes=[
            pltpu.VMEM((rows_total, pair, local_width), bf16),
            pltpu.VMEM((total_tokens, local_width), bf16),
            pltpu.VMEM((local_width // 128, 128), bf16),
            pltpu.VMEM((local_width // 128, 128), f32),
            pltpu.VMEM((total_tokens * groups, contraction), bf16),
            pltpu.VMEM((slots, 2, local_width, groups, head_dim), bf16),
            pltpu.VMEM((2, 2 * contraction, head_dim), bf16),
            pltpu.VMEM((out_weight.shape[0] * head_dim, local_width), bf16),
            pltpu.VMEM((2, 2, team * block, wide), f32),
            pltpu.VMEM((pieces, team * block, wide), bf16),
            pltpu.VMEM((pieces, team * block, wide), bf16),
            pltpu.VMEM((pieces, team, block, wide), bf16),
            pltpu.VMEM((pieces, team, block, wide), bf16),
            pltpu.VMEM((2, team * block, 128), f32),
            pltpu.VMEM((team * block, 128), f32),
            pltpu.VMEM((team, block, 128), f32),
            pltpu.VMEM((lanes, block, 128), f32),
            pltpu.VMEM((head_devices, group_size * block, head_dim), f32),
            pltpu.VMEM((head_devices, group_size * block, head_dim), f32),
            pltpu.VMEM((head_devices, block, group_size * head_dim), bf16),
            pltpu.VMEM((sources, block, group_size * head_dim), bf16),
            pltpu.VMEM((stretches, head_devices, share, across), bf16),
            pltpu.VMEM((stretches, head_devices, share, across), bf16),
            pltpu.VMEM((stretches, share, across), f32),
            dma((4,)),
            dma((slots, 2)),
            dma((2,)),
            dma((stretches,)),
            dma((2, pieces)),
            dma((pieces, team)),
            dma((pieces, team)),
            dma((2 + 2 * lanes,)),
            dma((team,)),
            dma((team,)),
            dma((team,)),
            dma((team,)),
            dma((stretches, head_devices)),
            dma((stretches, head_devices)),
        ],
        compiler_params=pltpu.CompilerParams(
            collective_id=0, has_side_effects=True, vmem_limit_bytes=63 << 20
        ),
    )(
        tokens,
        norm_gain.reshape(-1, 128),
        jnp.transpose(qkv_weight, (0, 2, 1, 3)),
        out_weight.reshape(-1, local_width),
        kv_cache.reshape(-1, head_dim),
        lengths,
        positions,
    )
    return got.reshape(share // pair, pair, local_width)


def body(tokens, norm_gain, qkv_weight, out_weight, kv_cache, lengths, positions):
    rows_local = kv_cache.shape[0]
    head_devices = lax.axis_size("gy")
    width_index = lax.axis_index("gx")
    head_index = lax.axis_index("gy")
    total_rows = tokens.shape[0]
    local_width = tokens.shape[2]
    groups_local = qkv_weight.shape[1]
    group_width = qkv_weight.shape[2]
    head_dim = qkv_weight.shape[3]
    group_size = group_width - 2
    block_rows = rows_local * head_devices
    places = lax.axis_size("gx")
    pair = tokens.shape[1]
    contraction = local_width * groups_local
    resident = (
        out_weight.size
        + 10 * contraction * head_dim
        + total_rows * pair * (2 * local_width + groups_local * contraction)
    )
    if (
        groups_local * rows_local * pair == 8
        and places % 2 == 0
        and head_devices > 1
        and total_rows == rows_local * places * head_devices
        and places % head_devices == 0
        and group_width % 2 == 0
        and head_dim == 128
        and kv_cache.shape[1] % 32 == 0
        and local_width % 512 == 0
        and 2 * resident < 59 << 20
    ):
        return whole_block(
            tokens, norm_gain, qkv_weight, out_weight, kv_cache, lengths, positions
        )
    tokens_wide = tokens.astype(jnp.float32)
    hidden = (tokens_wide * norm_gain.astype(jnp.float32)).astype(jnp.bfloat16)
    squares = jnp.sum(tokens_wide * tokens_wide, axis=-1)
    partial_value = jnp.dot(
        hidden.reshape(total_rows * 2, local_width),
        qkv_weight.reshape(local_width, -1),
        preferred_element_type=jnp.float32,
    )
    partial_value = partial_value.reshape(total_rows, 2, groups_local, group_width, head_dim)
    block_sum, block_squares = (
        lax.psum_scatter(partial_value, "gx", scatter_dimension=0, tiled=True),
        lax.psum_scatter(squares, "gx", scatter_dimension=0, tiled=True),
    )
    inv_rms = lax.rsqrt(block_squares / D + norm_eps)
    ready = finish(
        block_sum * inv_rms[:, :, None, None, None], positions, width_index * block_rows, block_rows
    )
    packed = lax.all_to_all(ready, "gy", split_axis=0, concat_axis=2, tiled=True)
    queries = packed[:, :, :, :group_size]
    key_new = packed[:, :, :, group_size]
    value_new = packed[:, :, :, group_size + 1]
    attended = attend(queries, key_new, value_new, kv_cache, lengths)
    regrouped = lax.all_to_all(attended, "gy", split_axis=2, concat_axis=0, tiled=True)
    out_flat = out_weight.reshape(-1, local_width)
    row_piece = lax.all_gather(regrouped, "gx", axis=0, tiled=True)
    piece_rows = row_piece.shape[0]
    product = jnp.dot(
        row_piece.reshape(piece_rows * 2, -1), out_flat, preferred_element_type=jnp.float32
    )
    terms = product.astype(jnp.bfloat16).reshape(head_devices, -1, 2, local_width)
    arrived = lax.all_to_all(terms, "gy", split_axis=0, concat_axis=0)
    own_sum = jnp.sum(arrived.astype(jnp.float32), axis=0)
    row_share = total_rows // head_devices
    residual = lax.dynamic_slice_in_dim(tokens, head_index * row_share, row_share, 0).astype(
        jnp.float32
    )
    return residual + own_sum


def solution(mesh):
    return jax.shard_map(
        body,
        mesh=mesh,
        in_specs=(
            P("groups", None, "gx"),
            P("gx"),
            P("gx", "gy", None, None),
            P("gy", None, "gx"),
            P(("groups", "gx", "gy"), None, None, None, None),
            P(("groups", "gx", "gy")),
            P("groups"),
        ),
        out_specs=P(("groups", "gy"), None, "gx"),
        check_vma=False,
    )
```

time: 102 us -> 68.9 us (0.68)
  Pallas kernels: 17.5 us -> 66.9 us
  waiting for transfers between devices: 27.6 us -> 0 us
  matrix products: 15.6 us -> 0 us
  blocking collectives: 14.8 us -> 0 us
  starting transfers between devices: 13.3 us -> 0 us
  local copies, waits for them, and re-layouts: 7.99 us -> 1.8 us
  other arithmetic: 4.58 us -> 0 us
    pallas_call x4 -> x1, Pallas kernels: 17.5 us -> 66.9 us  [whole_block(): pl.pallas_call(functools.partial(block_kernel, head_devices, places), out...]
    all_to_all x3 -> x0, waiting for transfers between devices: 27.6 us -> none  [the longest x1 15.2 us: body(): arrived = lax.all_to_all(terms, 'gy', split_axis=0, concat_axis=0)]
    dot_general x5 -> x0, matrix products: 15.6 us -> none  [the longest x1 13.6 us: body(): jnp.dot(row_piece.reshape(piece_rows * 2, -1), out_flat, preferred_elemen...]
    all_to_all x3 -> x0, starting transfers between devices: 13.3 us -> none  [the longest x1 5.53 us: body(): lax.all_to_all(ready, 'gy', split_axis=0, concat_axis=2, tiled=True)]
    all_to_all x1 -> x0, blocking collectives: 8.34 us -> none  [body(): lax.all_to_all(attended, 'gy', split_axis=2, concat_axis=0, tiled=True)]
    all_gather x1 -> x0, blocking collectives: 6.5 us -> none  [body(): row_piece = lax.all_gather(regrouped, 'gx', axis=0, tiled=True)]
    slice x4 -> x0, local copies, waits for them, and re-layouts: 3.38 us -> none  [the longest x1 3.25 us: attend(): cache_rows[:, :, 1]]
    add x2 -> x0, other arithmetic: 1.76 us -> none  [the longest x1 1.75 us: body(): return residual + own_sum]
  transfers between devices with their start and end apart: 3 -> 0, of which waited for: 3 -> 0; matrix products, arithmetic and copies ran while one was open for 4% -> 0% of each run, Pallas kernels for 0% -> 0%
where the time goes in v1:
time: 68.9 us; the launch traced here: 68.7 us
  Pallas kernels  66.9 us (97%)
  local copies, waits for them, and re-layouts  1.8 us (3%)
    pallas_call x1, Pallas kernels, whole_block(): pl.pallas_call(functools.partial(block_kernel, head_devices, places), out...  66.9 us
    reshape x1, local copies, waits for them, and re-layouts, whole_block(): return got.reshape(share // pair, pair, local_width)  1.8 us

profile of v1, /device:TPU:0, one launch (start us, length us, event | category | flops | bytes accessed | tf_op | source)
XLA Modules:
  0.0 68.7 jit_solution(6407323916203086071)
XLA Ops:
  0.0 66.9 %shard_map.73 = f32[16,4096]{1,0:T(8,128)} custom-call(bf16[32,2,4096]{2,1,0:T(2,128)(2,1)} %tokens_ref.1, bf16[32,128]{1,0:T(8,128)(2,1)} %bitcast.7, bf16[4096,18,2,128]{3,2,1,0:T(2,128)(2,1)} %bitcast.4, bf16[4096,4096]{1,0:T(8,128)(2,1)} %bitcast.5, bf16[12288,128]{1,0:T(8,128)(2,1)} %bitcast.6, s32[2]{0:T(128)} %lengths_ref.1, s32[32]{0:T(128)} %positions_ref.1), custom_call_target="tpu_custom_call" | custom-call | tf_op jit(solution)/shard_map/pallas_call | solution.py:652
  66.9 1.8 %reshape.15 = f32[8,2,4096]{2,1,0:T(2,128)} reshape(f32[16,4096]{1,0:T(8,128)} %shard_map.73) | data formatting | bytes 524288 | tf_op jit(solution)/shard_map/reshape | solution.py:709

commit v2 on v1

--- a/solution.py
+++ b/solution.py
@@ -1,4 +1,5 @@
 import functools
+import itertools
 import math
 
 import jax
@@ -95,7 +96,6 @@
     lengths_ref,
     positions_ref,
     out_ref,
-    raw,
     tok,
     gain,
     gain_wide,
@@ -135,7 +135,7 @@
     part_recvs,
 ):
     f32, bf16 = jnp.float32, jnp.bfloat16
-    rows_total, pair, local_width = raw.shape
+    rows_total, pair, local_width = tokens_ref.shape
     total_tokens = rows_total * pair
     columns, head_dim = qkv_ref.shape[1], qkv_ref.shape[3]
     groups = qkv_ref.shape[2]
@@ -171,7 +171,9 @@
             for at in range(2)
         ]
 
-    load_tokens = pltpu.make_async_copy(tokens_ref, raw, load_sems.at[0])
+    load_tokens = pltpu.make_async_copy(
+        tokens_ref.reshape(total_tokens, local_width), tok, load_sems.at[0]
+    )
     load_gain = pltpu.make_async_copy(gain_ref, gain, load_sems.at[1])
     load_tokens.start()
     load_gain.start()
@@ -204,14 +206,9 @@
     ).astype(bf16)
 
     load_tokens.wait()
-    retile = pltpu.make_async_copy(
-        raw.reshape(total_tokens, local_width), tok, load_sems.at[2]
-    )
-    retile.start()
     load_gain.wait()
     gain_wide[...] = gain[...].astype(f32)
-    retile.wait()
-    depth = 512
+    depth = 1024
 
     def widen(at, squares):
         start = pl.multiple_of(at * depth, depth)
@@ -319,8 +316,6 @@
         @pl.when(piece == pieces - 1)
         def _():
             load_cache.start()
-            for at in range(stretches):
-                weight_copy(at).start()
 
         for move in moves:
             move.wait()
@@ -369,6 +364,9 @@
 
     for off in range(1, lanes):
         square_send(off).start()
+    early = stretches // 2
+    for at in range(early):
+        weight_copy(at).start()
 
     stride = max_len + 16
     steps = 16
@@ -529,9 +527,14 @@
         att_hop(off).start()
     attended_recv[source_at] = attended_send[head]
     pair_hop(mine, core).start()
+    later = iter(range(early, stretches))
     for off in range(1, team):
+        for at in itertools.islice(later, 2):
+            weight_copy(at).start()
         att_arrival(off).wait_recv()
         pair_hop(lax.rem(mine + off, team), core).start()
+    for at in later:
+        weight_copy(at).start()
     for off in range(team):
         pair_hop(lax.rem(mine + off, team), 1 - core).wait_recv()
 
@@ -655,7 +658,6 @@
         in_specs=[hbm, hbm, hbm, hbm, hbm, smem, smem],
         out_specs=pl.BlockSpec(memory_space=pltpu.VMEM),
         scratch_shapes=[
-            pltpu.VMEM((rows_total, pair, local_width), bf16),
             pltpu.VMEM((total_tokens, local_width), bf16),
             pltpu.VMEM((local_width // 128, 128), bf16),
             pltpu.VMEM((local_width // 128, 128), f32),
@@ -738,7 +740,7 @@
         and group_width % 2 == 0
         and head_dim == 128
         and kv_cache.shape[1] % 32 == 0
-        and local_width % 512 == 0
+        and local_width % 1024 == 0
         and 2 * resident < 59 << 20
     ):
         return whole_block(

time: 68.9 us -> 60.3 us (0.88)
  Pallas kernels: 66.9 us -> 58.3 us
    pallas_call x1, Pallas kernels: 66.9 us -> 58.3 us  [whole_block(): pl.pallas_call(functools.partial(block_kernel, head_devices, places), out...]
where the time goes in v2:
time: 60.3 us; the launch traced here: 60.2 us
  Pallas kernels  58.3 us (97%)
  local copies, waits for them, and re-layouts  1.8 us (3%)
    pallas_call x1, Pallas kernels, whole_block(): pl.pallas_call(functools.partial(block_kernel, head_devices, places), out...  58.3 us
    reshape x1, local copies, waits for them, and re-layouts, whole_block(): return got.reshape(share // pair, pair, local_width)  1.8 us

profile of v2, /device:TPU:0, one launch (start us, length us, event | category | flops | bytes accessed | tf_op | source)
XLA Modules:
  0.0 60.2 jit_solution(3989945388741071187)
XLA Ops:
  0.0 58.3 %shard_map.73 = f32[16,4096]{1,0:T(8,128)} custom-call(bf16[32,2,4096]{2,1,0:T(2,128)(2,1)} %tokens_ref.1, bf16[32,128]{1,0:T(8,128)(2,1)} %bitcast.7, bf16[4096,18,2,128]{3,2,1,0:T(2,128)(2,1)} %bitcast.4, bf16[4096,4096]{1,0:T(8,128)(2,1)} %bitcast.5, bf16[12288,128]{1,0:T(8,128)(2,1)} %bitcast.6, s32[2]{0:T(128)} %lengths_ref.1, s32[32]{0:T(128)} %positions_ref.1), custom_call_target="tpu_custom_call" | custom-call | tf_op jit(solution)/shard_map/pallas_call | solution.py:655
  58.3 1.8 %reshape.15 = f32[8,2,4096]{2,1,0:T(2,128)} reshape(f32[16,4096]{1,0:T(8,128)} %shard_map.73) | data formatting | bytes 524288 | tf_op jit(solution)/shard_map/reshape | solution.py:711

commit v3 on v2

--- a/solution.py
+++ b/solution.py
@@ -275,7 +275,7 @@
 
     def pass_on(piece):
         core_hop(piece).wait_recv()
-        total = own_sum[lax.rem(piece, 2), core] + core_recv[piece].astype(f32)
+        total = own_sum[lax.rem(piece, 3), core] + core_recv[piece].astype(f32)
         row_send[piece] = total.reshape(row_send.shape[1:]).astype(bf16)
         row_recv[piece, mine] = row_send[piece, mine]
         for off in range(1, team):
@@ -299,6 +299,11 @@
     @pl.loop(0, pieces)
     def _(piece):
         slot, here = lax.rem(piece, slots), lax.rem(piece, 2)
+
+        @pl.when(piece == pieces - 1)
+        def _():
+            load_cache.start()
+
         for copy in bring(piece, slot):
             copy.wait()
         flat = ring.reshape(slots, 2, contraction, head_dim)
@@ -313,10 +318,6 @@
         for move in moves:
             move.start()
 
-        @pl.when(piece == pieces - 1)
-        def _():
-            load_cache.start()
-
         for move in moves:
             move.wait()
 
@@ -329,14 +330,16 @@
             [chunk[here, pl.ds(0, contraction)], chunk[here, pl.ds(contraction, contraction)]], axis=1
         )
         total = jnp.dot(left[...], right, preferred_element_type=f32)
-        own_sum[here] = total.reshape(own_sum.shape[1:])
-        core_send[piece] = own_sum[here, 1 - core].astype(bf16)
+        kept = lax.rem(piece, 3)
+        own_sum[kept] = total.reshape(own_sum.shape[1:])
+        core_send[piece] = own_sum[kept, 1 - core].astype(bf16)
         core_hop(piece).start()
 
-        @pl.when(piece >= 1)
+        @pl.when(piece >= 2)
         def _():
-            pass_on(piece - 1)
-
+            pass_on(piece - 2)
+
+    pass_on(pieces - 2)
     pass_on(pieces - 1)
     square_hop.wait_recv()
     square_mid[...] = (square_all[core] + square_core[...]).reshape(square_mid.shape)
@@ -607,7 +610,11 @@
         for off in range(1, head_devices):
             part_arrival(at, off).wait_recv()
             value = value + part_recv[at, lax.rem(head + off, head_devices)].astype(f32)
-        out_ref[:, span] = value
+        for row in range(share // pair):
+            for tile in range(across // 128):
+                out_ref[row, at * (across // 128) + tile] = value[
+                    row * pair : (row + 1) * pair, tile * 128 : (tile + 1) * 128
+                ]
 
     square_hop.wait_send()
     for off in range(1, lanes):
@@ -654,7 +661,7 @@
     dma = pltpu.SemaphoreType.DMA
     got = pl.pallas_call(
         functools.partial(block_kernel, head_devices, places),
-        out_shape=jax.ShapeDtypeStruct((share, local_width), f32),
+        out_shape=jax.ShapeDtypeStruct((share // pair, local_width // 128, pair, 128), f32),
         in_specs=[hbm, hbm, hbm, hbm, hbm, smem, smem],
         out_specs=pl.BlockSpec(memory_space=pltpu.VMEM),
         scratch_shapes=[
@@ -665,7 +672,7 @@
             pltpu.VMEM((slots, 2, local_width, groups, head_dim), bf16),
             pltpu.VMEM((2, 2 * contraction, head_dim), bf16),
             pltpu.VMEM((out_weight.shape[0] * head_dim, local_width), bf16),
-            pltpu.VMEM((2, 2, team * block, wide), f32),
+            pltpu.VMEM((3, 2, team * block, wide), f32),
             pltpu.VMEM((pieces, team * block, wide), bf16),
             pltpu.VMEM((pieces, team * block, wide), bf16),
             pltpu.VMEM((pieces, team, block, wide), bf16),
@@ -708,7 +715,7 @@
         lengths,
         positions,
     )
-    return got.reshape(share // pair, pair, local_width)
+    return jnp.transpose(got, (0, 2, 1, 3)).reshape(share // pair, pair, local_width)
 
 
 def body(tokens, norm_gain, qkv_weight, out_weight, kv_cache, lengths, positions):

time: 60.3 us -> 60.3 us (level)
    reshape x1 -> x0, local copies, waits for them, and re-layouts: 1.8 us -> none  [whole_block(): return got.reshape(share // pair, pair, local_width)]
    unnamed x0 -> x1, local copies, waits for them, and re-layouts: none -> 1.67 us
where the time goes in v3:
time: 60.3 us; the launch traced here: 60.2 us
  Pallas kernels  58.5 us (97%)
  local copies, waits for them, and re-layouts  1.67 us (3%)
    pallas_call x1, Pallas kernels, whole_block(): pl.pallas_call(functools.partial(block_kernel, head_devices, places), out...  58.5 us
    unnamed x1, local copies, waits for them, and re-layouts  1.67 us

profile of v3, /device:TPU:0, one launch (start us, length us, event | category | flops | bytes accessed | tf_op | source)
XLA Modules:
  0.0 60.2 jit_solution(12414383952279058375)
XLA Ops:
  0.0 58.5 %shard_map.73 = f32[8,32,2,128]{3,2,1,0:T(2,128)} custom-call(bf16[32,2,4096]{2,1,0:T(2,128)(2,1)} %tokens_ref.1, bf16[32,128]{1,0:T(8,128)(2,1)} %bitcast.11, bf16[4096,18,2,128]{3,2,1,0:T(2,128)(2,1)} %bitcast.7, bf16[4096,4096]{1,0:T(8,128)(2,1)} %bitcast.8, bf16[12288,128]{1,0:T(8,128)(2,1)} %bitcast.9, s32[2]{0:T(128)} %lengths_ref.1, s32[32]{0:T(128)} %positions_ref.1), custom_call_target="tpu_custom_call" | custom-call | tf_op jit(solution)/shard_map/pallas_call | solution.py:662
  58.5 1.7 %copy.9 = f32[8,2,4096]{2,1,0:T(2,128)} copy(f32[8,2,4096]{2,1,0:T(2,128)} %bitcast.10) | data formatting | bytes 524288

commit v4 on v3

--- a/solution.py
+++ b/solution.py
@@ -429,7 +429,35 @@
             row_arrival(piece, off).wait_recv()
 
     small = lax.broadcasted_iota(jnp.int32, (block, head_dim), 0)
-    for far in range(head_devices):
+    scale_factor = 1.0 / math.sqrt(head_dim)
+    count = pair * group_size
+    slot_id = lax.broadcasted_iota(jnp.int32, (count, stride), 1)
+    token_id = lax.broadcasted_iota(jnp.int32, (count, stride), 0) // group_size
+    fresh_seen = (slot_id >= max_len) & (slot_id - max_len <= token_id)
+
+    def send_to(far, at):
+        other = at * head_devices + far
+
+        @pl.when(other != mine)
+        def _():
+            hop(
+                attended_send.at[far],
+                attended_recv.at[source_at],
+                att_sends.at[other],
+                att_recvs.at[mine],
+                {"gx": at * 2 + core, "gy": far},
+            ).start()
+
+        @pl.when(other == mine)
+        def _():
+            attended_recv[source_at] = attended_send[far]
+
+    ends = [
+        far
+        for near_end in range((head_devices + 1) // 2)
+        for far in sorted({near_end, head_devices - 1 - near_end})
+    ]
+    for far in ends:
         for column in range(columns):
             piece, side = column // 2, column % 2
             value = row_recv[piece, far, :, side * head_dim : (side + 1) * head_dim].astype(f32)
@@ -456,42 +484,39 @@
                         chunk[cached_slot, pl.ds(base, 16)] = jnp.concatenate(
                             [fresh, jnp.zeros((16 - block, head_dim), f32)], axis=0
                         ).astype(bf16)
-
-    scale_factor = 1.0 / math.sqrt(head_dim)
-    count = pair * group_size
-    slot_id = lax.broadcasted_iota(jnp.int32, (count, stride), 1)
-    token_id = lax.broadcasted_iota(jnp.int32, (count, stride), 0) // group_size
-    fresh_seen = (slot_id >= max_len) & (slot_id - max_len <= token_id)
-    for row in range(rows_local):
-        seen = (slot_id < lengths_ref[row]) | fresh_seen
-        for every in range(all_groups):
-            far, group = every // groups, every % groups
-            first = group * near + row * pair
-            queries = jnp.concatenate(
-                [
-                    query_buf[far, pl.ds(first + token, group_size, stride=block), :]
-                    for token in range(pair)
-                ],
-                axis=0,
-            ).astype(bf16)
-            keys = chunk[cached_slot, pl.ds((row * kinds + every) * stride, stride)]
-            values = chunk[cached_slot, pl.ds((row * kinds + all_groups + every) * stride, stride)]
-            scores = lax.dot_general(
-                queries, keys, (((1,), (1,)), ((), ())), preferred_element_type=f32
-            )
-            scores = jnp.where(seen, scores * scale_factor, -1e30)
-            expo = jnp.exp(scores - jnp.max(scores, axis=1, keepdims=True))
-            weight = (expo / jnp.sum(expo, axis=1, keepdims=True)).astype(bf16)
-            result = jnp.dot(weight, values, preferred_element_type=f32)
-            for token in range(pair):
-                attended_buf[far, pl.ds(first + token, group_size, stride=block), :] = result[
-                    token * group_size : (token + 1) * group_size
+        for row in range(rows_local):
+            seen = (slot_id < lengths_ref[row]) | fresh_seen
+            for group in range(groups):
+                every = far * groups + group
+                first = group * near + row * pair
+                queries = jnp.concatenate(
+                    [
+                        query_buf[far, pl.ds(first + token, group_size, stride=block), :]
+                        for token in range(pair)
+                    ],
+                    axis=0,
+                ).astype(bf16)
+                keys = chunk[cached_slot, pl.ds((row * kinds + every) * stride, stride)]
+                values = chunk[
+                    cached_slot, pl.ds((row * kinds + all_groups + every) * stride, stride)
                 ]
-    for far in range(head_devices):
+                scores = lax.dot_general(
+                    queries, keys, (((1,), (1,)), ((), ())), preferred_element_type=f32
+                )
+                scores = jnp.where(seen, scores * scale_factor, -1e30)
+                expo = jnp.exp(scores - jnp.max(scores, axis=1, keepdims=True))
+                weight = (expo / jnp.sum(expo, axis=1, keepdims=True)).astype(bf16)
+                result = jnp.dot(weight, values, preferred_element_type=f32)
+                for token in range(pair):
+                    attended_buf[far, pl.ds(first + token, group_size, stride=block), :] = result[
+                        token * group_size : (token + 1) * group_size
+                    ]
         for at in range(group_size):
             attended_send[far, :, at * head_dim : (at + 1) * head_dim] = attended_buf[
                 far, at * block : (at + 1) * block, :
             ].astype(bf16)
+        for at in range(lanes):
+            send_to(far, at)
 
     def att_hop(off):
         other, place_of = member(off)
@@ -526,9 +551,6 @@
             partner,
         )
 
-    for off in range(team - 1, 0, -1):
-        att_hop(off).start()
-    attended_recv[source_at] = attended_send[head]
     pair_hop(mine, core).start()
     later = iter(range(early, stretches))
     for off in range(1, team):
@@ -635,6 +657,12 @@
     def _(at):
         for off in range(1, head_devices):
             part_hop(at, off).wait_send()
+
+
+def store_kernel(value_ref, out_ref, sem):
+    copy = pltpu.make_async_copy(value_ref, out_ref, sem.at[0])
+    copy.start()
+    copy.wait()
 
 
 def whole_block(tokens, norm_gain, qkv_weight, out_weight, kv_cache, lengths, positions):
@@ -704,7 +732,7 @@
             dma((stretches, head_devices)),
         ],
         compiler_params=pltpu.CompilerParams(
-            collective_id=0, has_side_effects=True, vmem_limit_bytes=63 << 20
+            collective_id=0, has_side_effects=True, vmem_limit_bytes=60 << 20
         ),
     )(
         tokens,
@@ -715,6 +743,13 @@
         lengths,
         positions,
     )
+    got = pl.pallas_call(
+        store_kernel,
+        out_shape=jax.ShapeDtypeStruct(got.shape, f32),
+        in_specs=[pl.BlockSpec(memory_space=pltpu.VMEM)],
+        out_specs=hbm,
+        scratch_shapes=[dma((1,))],
+    )(got)
     return jnp.transpose(got, (0, 2, 1, 3)).reshape(share // pair, pair, local_width)
 
 

time: 60.3 us -> 57.9 us (0.960)
  local copies, waits for them, and re-layouts: 1.67 us -> 0 us
  Pallas kernels: 58.5 us -> 57.8 us
    pallas_call x1, Pallas kernels: 58.5 us -> 56.1 us  [whole_block(): pl.pallas_call(functools.partial(block_kernel, head_devices, places), out...]
    unnamed x1 -> x0, local copies, waits for them, and re-layouts: 1.67 us -> none
    pallas_call x0 -> x1, Pallas kernels: none -> 1.66 us  [whole_block(): pl.pallas_call(store_kernel, out_shape=jax.ShapeDtypeStruct(got.shape, f3...]
where the time goes in v4:
time: 57.9 us; the launch traced here: 57.8 us
  Pallas kernels  57.8 us (100%)
    pallas_call x1, Pallas kernels, whole_block(): pl.pallas_call(functools.partial(block_kernel, head_devices, places), out...  56.1 us
    pallas_call x1, Pallas kernels, whole_block(): pl.pallas_call(store_kernel, out_shape=jax.ShapeDtypeStruct(got.shape, f3...  1.66 us

profile of v4, /device:TPU:0, one launch (start us, length us, event | category | flops | bytes accessed | tf_op | source)
XLA Modules:
  0.0 57.8 jit_solution(16232614209491760200)
XLA Ops:
  0.0 56.1 %shard_map.73.value_ref = f32[8,32,2,128]{3,2,1,0:T(2,128)} custom-call(bf16[32,2,4096]{2,1,0:T(2,128)(2,1)} %tokens_ref.1, bf16[32,128]{1,0:T(8,128)(2,1)} %bitcast.10, bf16[4096,18,2,128]{3,2,1,0:T(2,128)(2,1)} %bitcast.7, bf16[4096,4096]{1,0:T(8,128)(2,1)} %bitcast.8, bf16[12288,128]{1,0:T(8,128)(2,1)} %bitcast.9, s32[2]{0:T(128)} %lengths_ref.1, ...), custom_call_target="tpu_custom_call" | custom-call | tf_op jit(solution)/shard_map/pallas_call | solution.py:690
  56.1 1.7 %shard_map.74 = f32[8,32,2,128]{3,2,1,0:T(2,128)} custom-call(f32[8,32,2,128]{3,2,1,0:T(2,128)} %shard_map.73.value_ref), custom_call_target="tpu_custom_call" | custom-call | tf_op jit(solution)/shard_map/pallas_call | solution.py:746

commit v5 on v4

--- a/solution.py
+++ b/solution.py
@@ -367,7 +367,7 @@
 
     for off in range(1, lanes):
         square_send(off).start()
-    early = stretches // 2
+    early = stretches - stretches // 4
     for at in range(early):
         weight_copy(at).start()
 

time: 57.9 us -> 57.9 us (level)
  no operation moved by 1% of the time
where the time goes in v5:
time: 57.9 us; the launch traced here: 57.8 us
  Pallas kernels  57.8 us (100%)
    pallas_call x1, Pallas kernels, whole_block(): pl.pallas_call(functools.partial(block_kernel, head_devices, places), out...  56.1 us
    pallas_call x1, Pallas kernels, whole_block(): pl.pallas_call(store_kernel, out_shape=jax.ShapeDtypeStruct(got.shape, f3...  1.66 us

profile of v5, /device:TPU:0, one launch (start us, length us, event | category | flops | bytes accessed | tf_op | source)
XLA Modules:
  0.0 57.8 jit_solution(18357870503561507985)
XLA Ops:
  0.0 56.1 %shard_map.73.value_ref = f32[8,32,2,128]{3,2,1,0:T(2,128)} custom-call(bf16[32,2,4096]{2,1,0:T(2,128)(2,1)} %tokens_ref.1, bf16[32,128]{1,0:T(8,128)(2,1)} %bitcast.10, bf16[4096,18,2,128]{3,2,1,0:T(2,128)(2,1)} %bitcast.7, bf16[4096,4096]{1,0:T(8,128)(2,1)} %bitcast.8, bf16[12288,128]{1,0:T(8,128)(2,1)} %bitcast.9, s32[2]{0:T(128)} %lengths_ref.1, ...), custom_call_target="tpu_custom_call" | custom-call | tf_op jit(solution)/shard_map/pallas_call | solution.py:690
  56.1 1.7 %shard_map.74 = f32[8,32,2,128]{3,2,1,0:T(2,128)} custom-call(f32[8,32,2,128]{3,2,1,0:T(2,128)} %shard_map.73.value_ref), custom_call_target="tpu_custom_call" | custom-call | tf_op jit(solution)/shard_map/pallas_call | solution.py:746
